TPU v7x, 512 devices: a whole 4x4x16 slice. The times are simulated.
512 devices in a mesh: bond: 32 (over z_lo, x, core), leg: 16 (over z_hi, y).
Axes of the slice: x: 4, y: 4, z: 16 (z_hi: 4, z_lo: 4; z = z_hi * 4 + z_lo), core: 2. Of those that a mesh axis runs over, the one named last changes fastest.
Arguments:
- amplitudes: float32 [2, 1024, 262144], P(None, 'bond', 'leg'), may hold values from -6 to 6
- vectors: float32 [64, 262144], P(None, ('leg', 'bond')), may hold values from -0.01171875 to 0.01171875
- row_map: float32 [64, 4096], P('leg'), may hold values from -0.09375 to 0.09375
- col_map: float32 [64, 4096], P('bond'), may hold values from -0.09375 to 0.09375
Outputs:
- coarse: float32 [2, 8, 64, 64], P(None, None, 'leg', 'bond')
All inputs are finite; a program needn't handle non-finite values.
Results may differ from a plain program's by a relative error of at most 0.00014.
Values sent between devices are 32-bit elements; how exact they have to be, the bound alone decides.
A program may use at most 64 MiB of HBM per device.

v0:
```python
import jax
import jax.numpy as jnp
from jax import lax
from jax.sharding import PartitionSpec as P


def coarsen(slab, row_maps, col_maps):
    highest = lax.Precision.HIGHEST
    even = slab[:, 0::2]
    odd = slab[:, 1::2]
    inner = jnp.einsum("ztjc,qcd->ztqjd", even, col_maps, precision=highest)
    real_part = jnp.einsum("tqjd,tkd->tqjk", inner[0], odd[0], precision=highest) - jnp.einsum(
        "tqjd,tkd->tqjk", inner[1], odd[1], precision=highest
    )
    imag_part = jnp.einsum("tqjd,tkd->tqjk", inner[0], odd[1], precision=highest) + jnp.einsum(
        "tqjd,tkd->tqjk", inner[1], odd[0], precision=highest
    )
    paired = jnp.stack([real_part, imag_part])
    return jnp.einsum("pjk,ztqjk->ztpq", row_maps, paired, precision=highest)


def local(amplitudes, vectors, row_map, col_map):
    highest = lax.Precision.HIGHEST
    bond_dim = vectors.shape[0]
    partial_proj = jnp.einsum(
        "jk,zrk->zjr",
        lax.all_gather(vectors, "bond", axis=1, tiled=True),
        amplitudes,
        precision=highest,
    )
    summed = lax.psum(partial_proj, "leg")
    projected = lax.all_gather(summed, "bond", axis=2, tiled=True)
    slab_count = projected.shape[2] // bond_dim
    slab = projected.reshape(2, bond_dim, slab_count, bond_dim).transpose(0, 2, 1, 3)
    row_maps = row_map.reshape(row_map.shape[0], bond_dim, bond_dim)
    col_maps = col_map.reshape(col_map.shape[0], bond_dim, bond_dim)
    return coarsen(slab, row_maps, col_maps)


def solution(mesh):
    return jax.shard_map(
        local,
        mesh=mesh,
        in_specs=(
            P(None, "bond", "leg"),
            P(None, ("leg", "bond")),
            P("leg", None),
            P("bond", None),
        ),
        out_specs=P(None, None, "leg", "bond"),
        check_vma=False,
    )
```

profile of v0, /device:TPU:1, one launch (start us, length us, event | category | flops | bytes accessed | tf_op | source)
XLA Modules:
  0.0 250.0 jit_solution(4915478160259681730)
XLA Ops:
  6.5 0.0 all-gather.2.cloned.1.call-start
  6.5 0.7 all-gather.2.cloned.1.call-update
  7.3 0.9 reshape.14
  8.1 1.0 reshape.11
  9.1 73.8 %all-gather.2.cloned.1.call-done = f32[64,16384]{1,0:T(8,128)} async-done(((f32[64,512]{1,0:T(8,128)}), f32[64,16384]{1,0:T(8,128)}) %all-gather.2.cloned.1.call-update) | async-done | bytes 4194320 | tf_op jit(solution)/shard_map/all_gather | solution.py:27
  82.8 6.9 %fusion.4 = f32[2,64,32]{1,2,0:T(8,128)S(1)} fusion(f32[2,32,16384]{2,1,0:T(8,128)} %param.4, f32[64,16384]{1,0:T(8,128)} %all-gather.2.cloned.1.call-done), kind=kOutput, calls=%fused_computation.7 | convolution fusion | flops 805306368 | bytes 8404992 | tf_op jit(solution)/shard_map/jk,zrk->zjr/dot_general | solution.py:25
  89.8 84.2 %psum.7 = f32[2,64,32]{1,2,0:T(8,128)S(1)} all-reduce(f32[2,64,32]{1,2,0:T(8,128)S(1)} %fusion.4), channel_id=1, replica_groups=mesh['bond'=32,'leg'=16] {'leg'}, use_global_device_ids=true, to_apply=%region_0.0 | all-reduce | flops 4096 | bytes 32768 | tf_op jit(solution)/shard_map/psum | solution.py:31
  174.0 57.6 %all_gather.7 = f32[2,64,1024]{1,2,0:T(8,128)S(1)} all-gather(f32[2,64,32]{1,2,0:T(8,128)S(1)} %psum.7), channel_id=1, replica_groups=mesh['bond'=32,'leg'=16] {'bond'}, dimensions={2}, use_global_device_ids=true | all-gather | bytes 540672 | tf_op jit(solution)/shard_map/all_gather | solution.py:32
  231.5 0.3 copy.5
  231.9 1.0 convolution_bitcast_fusion
  232.9 0.6 fusion.10
  233.5 0.6 fusion.11
  234.1 0.6 fusion.2
  234.8 0.6 fusion.3
  235.4 0.1 pad_maximum_fusion
  235.5 7.0 %convolution_bitcast_fusion.1 = f32[2,8,4,2]{1,2,3,0:T(4,128)S(1)} fusion(f32[2,8,2,64,64]{4,3,2,1,0:T(8,128)S(1)} %pad_maximum_fusion, f32[4,64,64,1,1]{2,1,0,4,3:T(8,128)S(1)} %bitcast.55), kind=kOutput, calls=%fused_computation.8 | convolution fusion | flops 6291456 | bytes 590336 | tf_op jit(solution)/shard_map/pjk,ztqjk->ztpq/dot_general | solution.py:19
  242.5 0.6 copy.8
  (1 shorter events, 0.0 us)
Async XLA Ops:
  6.5 76.3 %all-gather.2.cloned.1.call-start = ((), (), s32[]{:S(2)}) async-start(), calls=%async_computation | async-start | bytes 4325376 | tf_op jit(solution)/shard_map/all_gather | solution.py:27
Sparse Core Ops, SparseCore 0:
  9.5 73.3 all-gather.1
where the time goes:
time: 250 us
  blocking collectives  142 us (57%)
  waiting for transfers between devices  74.5 us (30%)
  matrix products  17.4 us (7%)
  between operations  13.5 us (5%)
  local copies, waits for them, and re-layouts  2.82 us (1%)
    psum x1, blocking collectives, local(): summed = lax.psum(partial_proj, 'leg')  84.2 us
    all_gather x1, waiting for transfers between devices, local(): lax.all_gather(vectors, 'bond', axis=1, tiled=True)  73.8 us
    all_gather x1, blocking collectives, local(): projected = lax.all_gather(summed, 'bond', axis=2, tiled=True)  57.6 us
    dot_general x1, matrix products, coarsen(): return jnp.einsum('pjk,ztqjk->ztpq', row_maps, paired, precision=highest)  6.99 us
    dot_general x1, matrix products, local(): jnp.einsum('jk,zrk->zjr', lax.all_gather(vectors, 'bond', axis=1, tiled=T...  6.94 us
  transfers between devices with their start and end apart: 1, of which 1 were waited for; matrix products, arithmetic and copies ran while one was open for 1% of the time, Pallas kernels for 0%

commit v1 on v0

--- a/solution.py
+++ b/solution.py
@@ -24,7 +24,9 @@
     bond_dim = vectors.shape[0]
     partial_proj = jnp.einsum(
         "jk,zrk->zjr",
-        lax.all_gather(vectors, "bond", axis=1, tiled=True),
+        jnp.concatenate(
+            lax.all_to_all(jnp.stack([vectors] * lax.axis_size("bond")), "bond", 0, 0), axis=1
+        ),
         amplitudes,
         precision=highest,
     )

time: 250 us -> 284 us (1.14)
  waiting for transfers between devices: 74.5 us -> 92.9 us
  between operations: 13.5 us -> 0.09 us
  local copies, waits for them, and re-layouts: 2.82 us -> 16.1 us
  starting transfers between devices: 0.01 us -> 11.4 us
  blocking collectives: 142 us -> 145 us
    all_to_all x0 -> x1, waiting for transfers between devices: none -> 92.9 us  [local(): lax.all_to_all(jnp.stack([vectors] * lax.axis_size('bond')), 'bond', 0, 0)]
    all_gather x1 -> x0, waiting for transfers between devices: 73.8 us -> none  [local(): lax.all_gather(vectors, 'bond', axis=1, tiled=True)]
    reshape x0 -> x2, local copies, waits for them, and re-layouts: none -> 11.5 us  [local(): jnp.concatenate(lax.all_to_all(jnp.stack([vectors] * lax.axis_size('bond'...]
    all_to_all x0 -> x1, starting transfers between devices: none -> 11.4 us  [local(): lax.all_to_all(jnp.stack([vectors] * lax.axis_size('bond')), 'bond', 0, 0)]
    another operation x0 -> x1, local copies, waits for them, and re-layouts: none -> 3.39 us  [local(): jnp.stack([vectors] * lax.axis_size('bond'))]
  transfers between devices with their start and end apart: 1 -> 1, of which waited for: 1 -> 1; matrix products, arithmetic and copies ran while one was open for 1% -> 0% of each run, Pallas kernels for 0% -> 0%
where the time goes in v1:
time: 284 us; the launch traced here: 283 us
  blocking collectives  145 us (51%)
  waiting for transfers between devices  92.9 us (33%)
  matrix products  17.4 us (6%)
  local copies, waits for them, and re-layouts  16.1 us (6%)
  starting transfers between devices  11.4 us (4%)
    all_to_all x1, waiting for transfers between devices, local(): lax.all_to_all(jnp.stack([vectors] * lax.axis_size('bond')), 'bond', 0, 0)  92.9 us
    psum x1, blocking collectives, local(): summed = lax.psum(partial_proj, 'leg')  86.2 us
    all_gather x1, blocking collectives, local(): projected = lax.all_gather(summed, 'bond', axis=2, tiled=True)  59 us
    reshape x2, local copies, waits for them, and re-layouts, local(): jnp.concatenate(lax.all_to_all(jnp.stack([vectors] * lax.axis_size('bond'...  11.5 us
    all_to_all x1, starting transfers between devices, local(): lax.all_to_all(jnp.stack([vectors] * lax.axis_size('bond')), 'bond', 0, 0)  11.4 us
    dot_general x1, matrix products, coarsen(): return jnp.einsum('pjk,ztqjk->ztpq', row_maps, paired, precision=highest)  6.99 us
    dot_general x1, matrix products, local(): jnp.einsum('jk,zrk->zjr', jnp.concatenate(lax.all_to_all(jnp.stack([vecto...  6.93 us
  transfers between devices with their start and end apart: 1, of which 1 were waited for; matrix products, arithmetic and copies ran while one was open for 0% of the time, Pallas kernels for 0%

profile of v1, /device:TPU:1, one launch (start us, length us, event | category | flops | bytes accessed | tf_op | source)
XLA Modules:
  0.0 283.3 jit_solution(16803243802647067774)
XLA Ops:
  0.0 3.4 %stack.8 = f32[32,64,512]{2,1,0:T(8,128)} broadcast(f32[64,512]{1,0:T(8,128)} %param.5), dimensions={1,2} | broadcast | bytes 4325376 | tf_op jit(solution)/shard_map/stack | solution.py:28
  3.4 0.0 copy-start.1
  3.4 0.0 copy-start
  3.4 11.4 %all-to-all-start = ((f32[32,64,512]{2,1,0:T(8,128)}), f32[32,64,512]{2,1,0:T(8,128)}, u32[]{:S(2)}, u32[]{:S(2)}) async-start(f32[32,64,512]{2,1,0:T(8,128)} %stack.8), calls=%async_computation | async-start | bytes 8388608 | tf_op jit(solution)/shard_map/all_to_all | solution.py:28
  14.8 0.0 copy-done.1
  14.8 0.1 reshape.24
  14.9 0.0 copy-done
  14.9 0.1 reshape.21
  15.0 92.9 %all-to-all-done = f32[32,64,512]{2,1,0:T(8,128)} async-done(((f32[32,64,512]{2,1,0:T(8,128)}), f32[32,64,512]{2,1,0:T(8,128)}, u32[]{:S(2)}, u32[]{:S(2)}) %all-to-all-start) | async-done | bytes 4194336 | tf_op jit(solution)/shard_map/all_to_all | solution.py:28
  108.0 6.6 %copy.9 = f32[64,32,512]{2,1,0:T(8,128)} copy(f32[64,32,512]{2,0,1:T(8,128)} %bitcast) | data formatting | bytes 8388608 | tf_op jit(solution)/shard_map/reshape | solution.py:27
  114.5 4.9 %reshape.22 = f32[64,16384,1]{1,0,2:T(8,128)} reshape(f32[64,32,512]{2,1,0:T(8,128)} %copy.9) | data formatting | bytes 8388608 | tf_op jit(solution)/shard_map/reshape | solution.py:27
  119.5 6.9 %convolution_bitcast_fusion.1 = f32[2,64,32]{1,2,0:T(8,128)S(1)} fusion(f32[2,32,16384]{2,1,0:T(8,128)} %param.4, f32[64,16384,1]{1,0,2:T(8,128)} %reshape.22), kind=kOutput, calls=%fused_computation.5 | convolution fusion | flops 805306368 | bytes 8404992 | tf_op jit(solution)/shard_map/jk,zrk->zjr/dot_general | solution.py:25
  126.4 86.2 %psum.7 = f32[2,64,32]{1,2,0:T(8,128)S(1)} all-reduce(f32[2,64,32]{1,2,0:T(8,128)S(1)} %convolution_bitcast_fusion.1), channel_id=1, replica_groups=mesh['bond'=32,'leg'=16] {'leg'}, use_global_device_ids=true, to_apply=%region_0.0 | all-reduce | flops 4096 | bytes 32768 | tf_op jit(solution)/shard_map/psum | solution.py:33
  212.7 59.0 %all_gather.3 = f32[2,64,1024]{1,2,0:T(8,128)S(1)} all-gather(f32[2,64,32]{1,2,0:T(8,128)S(1)} %psum.7), channel_id=1, replica_groups=mesh['bond'=32,'leg'=16] {'bond'}, dimensions={2}, use_global_device_ids=true | all-gather | bytes 540672 | tf_op jit(solution)/shard_map/all_gather | solution.py:34
  271.7 0.3 copy.10
  272.1 1.0 convolution_bitcast_fusion
  273.0 0.6 fusion.6
  273.6 0.6 fusion.5
  274.3 0.6 fusion.1
  274.9 0.6 fusion
  275.6 0.1 pad_maximum_fusion
  275.7 7.0 %convolution_bitcast_fusion.2 = f32[2,8,4,2]{1,2,3,0:T(4,128)S(1)} fusion(f32[2,8,2,64,64]{4,3,2,1,0:T(8,128)S(1)} %pad_maximum_fusion, f32[4,64,64,1,1]{2,1,0,4,3:T(8,128)S(1)} %bitcast.52), kind=kOutput, calls=%fused_computation.6 | convolution fusion | flops 6291456 | bytes 590336 | tf_op jit(solution)/shard_map/pjk,ztqjk->ztpq/dot_general | solution.py:19
  282.7 0.6 copy.13
  (1 shorter events, 0.0 us)
Async XLA Ops:
  3.4 11.4 %copy-start.1 = (f32[2,4096]{1,0:T(2,128)S(1)}, f32[2,4096]{1,0:T(2,128)}, u32[]{:S(2)}) copy-start(f32[2,4096]{1,0:T(2,128)} %param.7) | copy-start | bytes 98308
  3.4 11.5 %copy-start = (f32[4,4096]{1,0:T(4,128)S(1)}, f32[4,4096]{1,0:T(4,128)}, u32[]{:S(2)}) copy-start(f32[4,4096]{1,0:T(4,128)} %param.6) | copy-start | bytes 196612
  3.4 104.6 %all-to-all-start = ((f32[32,64,512]{2,1,0:T(8,128)}), f32[32,64,512]{2,1,0:T(8,128)}, u32[]{:S(2)}, u32[]{:S(2)}) async-start(f32[32,64,512]{2,1,0:T(8,128)} %stack.8), calls=%async_computation | async-start | bytes 8388608 | tf_op jit(solution)/shard_map/all_to_all | solution.py:28
